TPU v7x, 512 devices: a whole 4x8x8 slice. The times are simulated.
512 devices in a mesh: dp: 16 (over y, core), seq: 32 (over z, x).
Axes of the slice: x: 4, y: 8, z: 8, core: 2. Of those that a mesh axis runs over, the one named last changes fastest.
Arguments:
- hidden: bfloat16 [65536, 2048], P(('dp', 'seq')), may hold values from -6 to 6
- queries: bfloat16 [65536, 2048], P(('dp', 'seq')), may hold values from -360 to 360
- values: bfloat16 [65536, 512], P(('dp', 'seq')), may hold values from -6 to 6
- row_target: int32 [65536], P(('dp', 'seq')), may hold values from 0 to 4095, as said below
- key_weight: bfloat16 [2048, 512], P(('dp', 'seq')), may hold values from -0.125 to 0.125
- dialogue_lengths: int32 [16, 64], P('dp'), may hold values from 1 to 256, 4096 in all within a row
- teacher_pick: int32 [65536, 128], P(('dp', 'seq')), may hold values from 0 to 65279
- teacher_prob: float32 [65536, 128], P(('dp', 'seq')), may hold values from 0.02 to 1
Outputs:
- attn_out: bfloat16 [65536, 2048], P(('dp', 'seq'))
- token_loss: float32 [65536], P(('dp', 'seq'))
- weight_grad: float32 [2048, 512], P(('dp', 'seq'))
Inputs may be any that keep to these rules, and one draw needn't show every extreme that they name: Within each pack, row_target holds every position 0 to 4095 once. Of the 128 rows of one device, at most 6 have targets in one block of 128 positions (target // 128 names the block), and in every draw some device sends exactly 6 to some block.
All inputs are finite; a program needn't handle non-finite values.
Results may differ from a plain program's by a relative error of at most 0.012.
The roundings to bfloat16 on the way count: a program that leaves them out, or rounds other values in their place, can miss the bound.
Values may be sent and summed in bfloat16 or wider, within the bound.
No kernel may reach another device: no remote copies, remote signals or barrier semaphores. Data moves between devices by JAX's collectives and lax.ppermute only.
A program may use at most 64 MiB of HBM per device.

v0:
```python
import jax
import jax.numpy as jnp
from jax import lax
from jax.sharding import PartitionSpec as P

HEAD_DIM = 128
SPAN = 2


negative = -1e30
rope_base = 500000.0


def side_by_side(arrays, axis, split_dim, concat_dim, along):
    ends, at = ([], 0)
    for a in arrays[:-1]:
        at += a.shape[along]
        ends.append(at)
    both = jnp.concatenate(arrays, axis=along)
    return tuple(
        jnp.split(
            lax.all_to_all(both, axis, split_axis=split_dim, concat_axis=concat_dim, tiled=True),
            ends,
            axis=along,
        )
    )


def shifted(shard, axis, by):
    devices = lax.axis_size(axis)
    pairs = [(i, i + by) for i in range(devices) if 0 <= i + by < devices]
    return lax.ppermute(shard, axis, pairs)


def rotate(matrix, positions, direction):
    count = matrix.shape[0]
    split = matrix.reshape(count, -1, HEAD_DIM)
    halfway = HEAD_DIM // 2
    frequency = rope_base ** (-2.0 * jnp.arange(halfway, dtype=jnp.float32) / HEAD_DIM)
    angle = positions.astype(jnp.float32)[:, None] * frequency[None, :]
    cosine = jnp.cos(angle)[:, None, :]
    sine = direction * jnp.sin(angle)[:, None, :]
    first_half = split[..., :halfway]
    second_half = split[..., halfway:]
    joined = jnp.concatenate(
        [first_half * cosine - second_half * sine, second_half * cosine + first_half * sine],
        axis=-1,
    )
    return joined.reshape(count, -1)


def dialogue_starts(lengths, positions):
    ending = jnp.cumsum(lengths)
    picked = jnp.where(ending[None, :] <= positions[:, None], lengths[None, :], 0)
    return jnp.sum(picked, axis=1)


def block_targets(label_index, label_prob, key_start, width):
    within = label_index - key_start
    columns = jnp.arange(width, dtype=jnp.int32)
    matches = within[..., None] == columns[None, None, None, :]
    table = jnp.sum(jnp.where(matches, label_prob[..., None], 0.0), axis=2)
    return jnp.transpose(table, (1, 0, 2))


def project_keys(inputs, key_weight):
    return jnp.dot(
        inputs,
        lax.all_gather(key_weight, ("dp", "seq"), axis=0, tiled=True),
        preferred_element_type=jnp.float32,
    )


def move_rows(first_rows, second_rows, third_rows, row_places):
    return (
        *side_by_side((first_rows, second_rows, third_rows), "seq", 0, 0, 1),
        lax.all_to_all(row_places, "seq", split_axis=0, concat_axis=0, tiled=True),
    )


def guarded(compute, operands):
    return compute(*operands)


def local(
    hidden, queries, values, row_target, key_weight, dialogue_lengths, teacher_pick, teacher_prob
):
    local_rows = hidden.shape[0]
    seq_count = lax.axis_size("seq")
    seq_index = lax.axis_index("seq")
    device_count = seq_count * lax.axis_size("dp")
    capacity = local_rows // seq_count + local_rows // (2 * seq_count)
    head_count = queries.shape[1] // HEAD_DIM
    kv_count = values.shape[1] // HEAD_DIM
    group_size = head_count // kv_count
    top_count = teacher_pick.shape[1] // head_count
    scaling = HEAD_DIM ** (-0.5)
    destination = row_target // local_rows
    offset_in = row_target - destination * local_rows
    one_hot = (destination[:, None] == jnp.arange(seq_count, dtype=jnp.int32)[None, :]).astype(
        jnp.int32
    )
    rank_in = jnp.sum((jnp.cumsum(one_hot, axis=0) - one_hot) * one_hot, axis=1)
    slot_of = destination * capacity + rank_in

    def parcel(data, filler):
        holder = jnp.full((seq_count * capacity,) + data.shape[1:], filler, data.dtype)
        return holder.at[slot_of].set(data)

    def settle(data, places):
        holder = jnp.zeros((local_rows,) + data.shape[1:], data.dtype)
        return holder.at[places].set(data, mode="drop")

    positions = seq_index * local_rows + jnp.arange(local_rows, dtype=jnp.int32)
    received = move_rows(
        parcel(hidden, 0), parcel(queries, 0), parcel(values, 0), parcel(offset_in, local_rows)
    )
    hidden_seq = settle(received[0], received[3])
    queries_seq = settle(received[1], received[3])
    values_seq = settle(received[2], received[3])
    keys_seq = rotate(project_keys(hidden_seq, key_weight), positions, 1.0).astype(jnp.bfloat16)
    starts = dialogue_starts(dialogue_lengths[0], positions)
    reach = (positions - starts + 1)[:, None]
    label_index = (starts[:, None] + teacher_pick % reach).reshape(
        local_rows, head_count, top_count
    )
    label_prob = teacher_prob.reshape(local_rows, head_count, top_count)
    target_mass = jnp.sum(label_prob, axis=2).T.reshape(kv_count, group_size, local_rows)
    entropy = jnp.sum(label_prob * jnp.log(label_prob), axis=(1, 2))
    query_heads = queries_seq.reshape(local_rows, kv_count, group_size, HEAD_DIM)
    earliest = jnp.min(starts)
    blocks = [(keys_seq, values_seq)]
    for distance in range(1, SPAN + 1):
        blocks.append(shifted((keys_seq, values_seq), "seq", distance))

    def scores_of(key_block, key_start):
        key_heads = key_block.reshape(local_rows, kv_count, HEAD_DIM)
        score = (
            jnp.einsum("tkgd,wkd->kgtw", query_heads, key_heads, preferred_element_type=jnp.float32)
            * scaling
        )
        key_pos = key_start + jnp.arange(local_rows, dtype=jnp.int32)
        allowed = (key_pos[None, :] >= starts[:, None]) & (key_pos[None, :] <= positions[:, None])
        held = jnp.where(allowed[None, None], score, negative)
        table = block_targets(label_index, label_prob, key_start, local_rows)
        return (score, held, table.reshape(kv_count, group_size, local_rows, local_rows))

    def first_pass(key_block, key_start):
        score, held, table = scores_of(key_block, key_start)
        block_top = jnp.max(held, axis=-1)
        block_total = jnp.sum(jnp.exp(held - block_top[..., None]), axis=-1)
        return (block_top, block_total, jnp.sum(table * score, axis=-1))

    tops, totals, pickings, alive_list = ([], [], [], [])
    for distance, (key_block, value_block) in enumerate(blocks):
        key_start = (seq_index - distance) * local_rows
        alive = earliest < key_start + local_rows
        alive_list.append((alive, key_start))
        block_top, block_total, picking = guarded(first_pass, (key_block, key_start))
        tops.append(block_top)
        totals.append(block_total)
        pickings.append(picking)
    top_all = jnp.max(jnp.stack(tops), axis=0)
    total_all = jnp.sum(jnp.stack(totals) * jnp.exp(jnp.stack(tops) - top_all[None]), axis=0)
    lse = top_all + jnp.log(total_all)
    picked_all = jnp.sum(jnp.stack(pickings), axis=0)
    token_loss = (
        entropy - jnp.sum(picked_all, axis=(0, 1)) + jnp.sum(target_mass * lse, axis=(0, 1))
    ) / head_count

    def second_pass(key_block, value_block, key_start):
        score, held, table = scores_of(key_block, key_start)
        weight = jnp.exp(held - lse[..., None])
        value_heads = value_block.reshape(local_rows, kv_count, HEAD_DIM)
        partial_value = jnp.einsum(
            "kgtw,wkd->tkgd",
            weight.astype(jnp.bfloat16),
            value_heads,
            preferred_element_type=jnp.float32,
        )
        slope = ((weight * target_mass[..., None] - table) / head_count).astype(jnp.bfloat16)
        gradient = (
            jnp.einsum("kgtw,tkgd->wkd", slope, query_heads, preferred_element_type=jnp.float32)
            * scaling
        )
        return (partial_value, gradient.reshape(local_rows, kv_count * HEAD_DIM))

    output_sum = jnp.zeros((local_rows, kv_count, group_size, HEAD_DIM), jnp.float32)
    block_grads = []
    for distance, (key_block, value_block) in enumerate(blocks):
        alive, key_start = alive_list[distance]
        partial_value, gradient = guarded(second_pass, (key_block, value_block, key_start))
        output_sum = output_sum + partial_value
        block_grads.append(gradient)
    attn_out = output_sum.astype(jnp.bfloat16).reshape(local_rows, head_count * HEAD_DIM)
    rotated_grad = block_grads[0]
    for distance in range(1, SPAN + 1):
        rotated_grad = rotated_grad + shifted(
            block_grads[distance].astype(jnp.bfloat16), "seq", -distance
        ).astype(jnp.float32)
    key_grad = rotate(rotated_grad, positions, -1.0).astype(jnp.bfloat16)
    inverse_root = (local_rows * device_count) ** (-0.5)
    weight_grad = lax.psum_scatter(
        jnp.einsum("td,tc->dc", hidden_seq, key_grad, preferred_element_type=jnp.float32)
        * inverse_root,
        ("dp", "seq"),
        scatter_dimension=0,
        tiled=True,
    )
    return (attn_out, token_loss, weight_grad)


def solution(mesh):
    placed = (
        P(("dp", "seq"), None),
        P(("dp", "seq"), None),
        P(("dp", "seq"), None),
        P(("dp", "seq")),
        P(("dp", "seq"), None),
        P("dp", None),
        P(("dp", "seq"), None),
        P(("dp", "seq"), None),
    )
    return jax.shard_map(
        local,
        mesh=mesh,
        in_specs=placed,
        out_specs=(P(("dp", "seq"), None), P(("dp", "seq")), P(("dp", "seq"), None)),
        check_vma=False,
    )
```

profile of v0, /device:TPU:24, one launch (start us, length us, event | category | flops | bytes accessed | tf_op | source)
XLA Modules:
  0.0 468.3 jit_solution(1909932500916336995)
XLA Ops:
  7.2 0.7 all-gather.3.cloned.1.call-update
  7.9 0.7 multiply_subtract_fusion.1
  9.0 1.0 scatter_custom_fusion
  10.0 0.7 all_to_all.16
  10.7 13.2 %all-to-all-start = ((s32[32,6,1]{1,2,0:T(1,128)}), s32[32,6,1]{1,2,0:T(1,128)S(1)}, u32[]{:S(2)}, u32[]{:S(2)}) async-start(s32[32,6,1]{1,2,0:T(1,128)} %bitcast), calls=%async_computation | async-start | bytes 32768 | tf_op jit(solution)/shard_map/all_to_all | solution.py:77
  23.9 1.5 scatter_custom_fusion.3
  25.4 2.1 scatter_custom_fusion.2
  27.5 2.1 scatter_custom_fusion.1
  29.8 1.7 all_to_all.19
  31.5 2.1 all-to-all-done
  33.6 7.8 %all-to-all-start.1 = ((bf16[32,6,4608]{2,1,0:T(8,128)(2,1)}), bf16[32,6,4608]{2,1,0:T(8,128)(2,1)S(1)}, u32[]{:S(2)}, u32[]{:S(2)}) async-start(bf16[32,6,4608]{2,1,0:T(8,128)(2,1)} %all_to_all.19), calls=%async_computation.1 | async-start | bytes 4718592 | tf_op jit(solution)/shard_map/all_to_all | solution.py:22
  41.5 0.5 iota_add_fusion.2
  42.5 1.3 subtract_bitcast_fusion.2
  44.4 1.4 copy.109
  45.8 2.2 copy.113
  48.1 2.2 copy.107
  50.3 13.4 %select_reduce_fusion.1 = (f32[128,16,128]{2,1,0:T(8,128)}, f32[128,16,128]{2,1,0:T(8,128)}, f32[128,16,128]{2,1,0:T(8,128)}) fusion(s32[128,16,8]{2,1,0:T(8,128)S(1)} %copy.111, f32[128,16,8]{2,1,0:T(8,128)} %copy.109, s32[128,16,8]{2,1,0:T(8,128)} %copy.113, s32[128,16,8]{2,1,0:T(8,128)} %copy.107), kind=kLoop, calls=%fused_computation.9 | loop fusion | flops 18087936 | bytes 3407872 | tf_op jit(solution)/shard_map/reduce_sum | solution.py:62
  63.6 2.6 copy.114
  66.3 2.6 copy.112
  68.8 1.4 copy.110
  70.5 1.0 broadcast_multiply_fusion
  72.0 0.7 reduce.12
  72.8 25.2 %all-to-all-done.1 = bf16[32,6,4608]{2,1,0:T(8,128)(2,1)S(1)} async-done(((bf16[32,6,4608]{2,1,0:T(8,128)(2,1)}), bf16[32,6,4608]{2,1,0:T(8,128)(2,1)S(1)}, u32[]{:S(2)}, u32[]{:S(2)}) %all-to-all-start.1) | async-done | bytes 1769504 | tf_op jit(solution)/shard_map/all_to_all | solution.py:22
  98.0 1.6 all_to_all.21
  99.6 2.6 scatter_custom_fusion.6
  102.2 2.4 scatter_custom_fusion.5
  104.9 31.5 %all-gather.3.cloned.1.call-done = bf16[512,4,512]{2,1,0:T(4,128)(2,1)} async-done(((bf16[1,4,512]{2,1,0:T(4,128)(2,1)}), bf16[512,4,512]{2,1,0:T(4,128)(2,1)}) %all-gather.3.cloned.1.call-update) | async-done | bytes 2097168 | tf_op jit(solution)/shard_map/all_gather | solution.py:69
  136.5 4.0 reshape.528
  140.4 2.1 fusion.77
  143.2 4.5 collective-permute-start.1
  147.7 2.7 collective-permute-start
  151.7 2.0 collective-permute-done
  154.4 0.9 multiply_reduce_fusion.1
  156.3 1.3 collective-permute-start.5
  157.6 1.3 collective-permute-start.4
  159.4 6.5 %collective-permute-done.5 = bf16[128,512]{0,1:T(8,128)(2,1)S(1)} collective-permute-done((bf16[128,512]{0,1:T(8,128)(2,1)S(1)}, bf16[128,512]{0,1:T(8,128)(2,1)S(1)}, u32[]{:S(2)}, u32[]{:S(2)}) %collective-permute-start.5) | collective-permute-done | bytes 131104 | tf_op jit(solution)/shard_map/ppermute | solution.py:32
  165.9 2.1 collective-permute-done.4
  168.7 2.7 convolution_multiply_fusion
  171.4 1.8 scatter_custom_fusion.4
  173.2 4.5 collective-permute-start.2
  177.7 6.0 %collective-permute-start.3 = (bf16[128,512]{1,0:T(8,128)(2,1)S(1)}, bf16[128,512]{1,0:T(8,128)(2,1)}, u32[]{:S(2)}, u32[]{:S(2)}) collective-permute-start(bf16[128,512]{1,0:T(8,128)(2,1)S(1)} %scatter_custom_fusion.4), channel_id=1, source_target_pairs={{0,2},{1,3},{2,4},{3,5},{4,6},{5,7},{6,8},{7,9},{8,10},{9,11},{10,... | collective-permute-start | bytes 393224 | tf_op jit(solution)/shard_map/ppermute | solution.py:32
  183.6 0.6 fusion.56
  184.4 1.7 copy.102
  186.1 1.0 copy.104
  187.5 1.3 convolution_add_fusion.1
  189.1 1.0 copy.124
  190.7 269.5 %all-reduce.3.cloned.1.call-done = f32[2048,512]{1,0:T(8,128)} async-done(((f32[2048,512]{1,0:T(8,128)}), f32[2048,512]{1,0:T(8,128)}) %all-reduce.3.cloned.1.call-update) | async-done | bytes 4194320
  460.1 1.3 constant_dynamic-slice_fusion
  (92 shorter events, 8.8 us)
Async XLA Ops:
  7.2 129.3 %all-gather.3.cloned.1.call-start = ((), (), s32[]{:S(2)}) async-start(), calls=%async_computation.2 | async-start | bytes 2101248 | tf_op jit(solution)/shard_map/all_gather | solution.py:69
  10.7 22.9 %all-to-all-start = ((s32[32,6,1]{1,2,0:T(1,128)}), s32[32,6,1]{1,2,0:T(1,128)S(1)}, u32[]{:S(2)}, u32[]{:S(2)}) async-start(s32[32,6,1]{1,2,0:T(1,128)} %bitcast), calls=%async_computation | async-start | bytes 32768 | tf_op jit(solution)/shard_map/all_to_all | solution.py:77
  29.7 12.2 %copy-start.15 = (s32[1,64]{1,0:T(1,128)S(1)}, s32[1,64]{1,0:T(1,128)}, u32[]{:S(2)}) copy-start(s32[1,64]{1,0:T(1,128)} %param.13) | copy-start | bytes 772
  29.8 12.5 %copy-start.9 = (s32[128,128]{1,0:T(8,128)S(1)}, s32[128,128]{1,0:T(8,128)}, u32[]{:S(2)}) copy-start(s32[128,128]{1,0:T(8,128)} %param.14) | copy-start | bytes 196612
  31.5 12.8 %copy-start.7 = (f32[128,128]{1,0:T(8,128)S(1)}, f32[128,128]{1,0:T(8,128)}, u32[]{:S(2)}) copy-start(f32[128,128]{1,0:T(8,128)} %param.15) | copy-start | bytes 196612
  33.6 64.4 %all-to-all-start.1 = ((bf16[32,6,4608]{2,1,0:T(8,128)(2,1)}), bf16[32,6,4608]{2,1,0:T(8,128)(2,1)S(1)}, u32[]{:S(2)}, u32[]{:S(2)}) async-start(bf16[32,6,4608]{2,1,0:T(8,128)(2,1)} %all_to_all.19), calls=%async_computation.1 | async-start | bytes 4718592 | tf_op jit(solution)/shard_map/all_to_all | solution.py:22
  41.4 418.7 %all-reduce.3.cloned.1.call-start = ((), (), s32[]{:S(2)}) async-start(), calls=%async_computation.3 | async-start | bytes 8388608
  42.0 1.9 copy-start.13
  42.5 1.3 copy-start.11
  63.6 5.2 %copy-start.6 = (f32[128,16,128]{2,1,0:T(8,128)S(1)}, f32[128,16,128]{2,1,0:T(8,128)}, u32[]{:S(2)}) copy-start(f32[128,16,128]{2,1,0:T(8,128)} %get-tuple-element.19) | copy-start | bytes 3145732
  63.6 6.7 %copy-start.12 = (s32[128]{0:T(128)S(1)}, s32[128]{0:T(128)}, u32[]{:S(2)}) copy-start(s32[128]{0:T(128)} %copy-done.11) | copy-start | bytes 1540
  63.6 6.7 %copy-start.14 = (s32[128]{0:T(128)S(1)}, s32[128]{0:T(128)}, u32[]{:S(2)}) copy-start(s32[128]{0:T(128)} %copy-done.13) | copy-start | bytes 1540
  72.8 32.2 %copy-start.17 = (s32[192,1]{0,1:T(1,128)}, s32[192,1]{0,1:T(1,128)S(1)}, u32[]{:S(2)}) copy-start(s32[192,1]{0,1:T(1,128)S(1)} %compare_select_fusion) | copy-start | bytes 2308
  140.4 10.3 %copy-start.4 = (f32[16,128,128]{1,2,0:T(8,128)S(1)}, f32[16,128,128]{1,2,0:T(8,128)}, u32[]{:S(2)}) copy-start(f32[16,128,128]{1,2,0:T(8,128)} %copy.110) | copy-start | bytes 3145732
  143.2 8.1 %collective-permute-start.1 = (bf16[128,512]{0,1:T(8,128)(2,1)S(1)}, bf16[128,512]{0,1:T(8,128)(2,1)S(1)}, u32[]{:S(2)}, u32[]{:S(2)}) collective-permute-start(bf16[128,512]{0,1:T(8,128)(2,1)S(1)} %bitcast.171), channel_id=1, source_target_pairs={{0,2},{1,3},{2,4},{3,5},{4,6},{5,7},{6,8},{7,9},{8,10},{9,11},{10,... | collective-permute-start | bytes 393224 | tf_op jit(solution)/shard_map/ppermute | solution.py:32
  147.7 5.9 %collective-permute-start = (bf16[128,512]{0,1:T(8,128)(2,1)S(1)}, bf16[128,512]{0,1:T(8,128)(2,1)S(1)}, u32[]{:S(2)}, u32[]{:S(2)}) collective-permute-start(bf16[128,512]{0,1:T(8,128)(2,1)S(1)} %bitcast.172), channel_id=1, source_target_pairs={{0,1},{1,2},{2,3},{3,4},{4,5},{5,6},{6,7},{7,8},{8,9},{9,10},{10,1... | collective-permute-start | bytes 393224 | tf_op jit(solution)/shard_map/ppermute | solution.py:32
  150.4 3.6 copy-start.2
  150.7 8.2 %copy-start = (f32[4,4,128,128]{2,3,1,0:T(8,128)}, f32[4,4,128,128]{2,3,1,0:T(8,128)S(1)}, u32[]{:S(2)}) copy-start(f32[4,4,128,128]{2,3,1,0:T(8,128)S(1)} %get-tuple-element.48) | copy-start | bytes 3145732
  150.8 3.6 copy-start.3
  154.4 4.5 copy-start.5
  156.3 9.6 %collective-permute-start.5 = (bf16[128,512]{0,1:T(8,128)(2,1)S(1)}, bf16[128,512]{0,1:T(8,128)(2,1)S(1)}, u32[]{:S(2)}, u32[]{:S(2)}) collective-permute-start(bf16[128,512]{0,1:T(8,128)(2,1)S(1)} %bitcast.170), channel_id=1, source_target_pairs={{2,0},{3,1},{4,2},{5,3},{6,4},{7,5},{8,6},{9,7},{10,8},{11,9},{12,... | collective-permute-start | bytes 393224 | tf_op jit(solution)/shard_map/ppermute | solution.py:32
  157.6 10.4 %collective-permute-start.4 = (bf16[128,512]{0,1:T(8,128)(2,1)S(1)}, bf16[128,512]{0,1:T(8,128)(2,1)S(1)}, u32[]{:S(2)}, u32[]{:S(2)}) collective-permute-start(bf16[128,512]{0,1:T(8,128)(2,1)S(1)} %bitcast.169), channel_id=1, source_target_pairs={{1,0},{2,1},{3,2},{4,3},{5,4},{6,5},{7,6},{8,7},{9,8},{10,9},{11,1... | collective-permute-start | bytes 393224 | tf_op jit(solution)/shard_map/ppermute | solution.py:32
  168.6 15.0 %copy-start.8 = (f32[128,128]{1,0:T(8,128)S(1)}, f32[128,128]{1,0:T(8,128)}, u32[]{:S(2)}) copy-start(f32[128,128]{1,0:T(8,128)} %param.15) | copy-start | bytes 196612
  171.4 15.8 %copy-start.1 = (f32[4,4,128,128]{2,3,1,0:T(8,128)S(1)}, f32[4,4,128,128]{2,3,1,0:T(8,128)}, u32[]{:S(2)}) copy-start(f32[4,4,128,128]{2,3,1,0:T(8,128)} %copy-done) | copy-start | bytes 3145732
  173.2 11.2 %collective-permute-start.2 = (bf16[128,512]{1,0:T(8,128)(2,1)S(1)}, bf16[128,512]{1,0:T(8,128)(2,1)}, u32[]{:S(2)}, u32[]{:S(2)}) collective-permute-start(bf16[128,512]{1,0:T(8,128)(2,1)S(1)} %scatter_custom_fusion.4), channel_id=1, source_target_pairs={{0,1},{1,2},{2,3},{3,4},{4,5},{5,6},{6,7},{7,8},{8,9},{9,10},{10,1... | collective-permute-start | bytes 393224 | tf_op jit(solution)/shard_map/ppermute | solution.py:32
  177.7 8.4 %collective-permute-start.3 = (bf16[128,512]{1,0:T(8,128)(2,1)S(1)}, bf16[128,512]{1,0:T(8,128)(2,1)}, u32[]{:S(2)}, u32[]{:S(2)}) collective-permute-start(bf16[128,512]{1,0:T(8,128)(2,1)S(1)} %scatter_custom_fusion.4), channel_id=1, source_target_pairs={{0,2},{1,3},{2,4},{3,5},{4,6},{5,7},{6,8},{7,9},{8,10},{9,11},{10,... | collective-permute-start | bytes 393224 | tf_op jit(solution)/shard_map/ppermute | solution.py:32
  187.5 2.7 copy-start.10
  187.5 2.7 copy-start.16
Sparse Core Ops, SparseCore 0:
  12.2 124.2 all-gather.2
  171.5 288.5 all-reduce.2
where the time goes:
time: 469 us; the launch traced here: 468 us
  waiting for transfers between devices  340 us (72%)
  local copies, waits for them, and re-layouts  41.6 us (9%)
  starting transfers between devices  41.3 us (9%)
  other arithmetic  21.7 us (5%)
  between operations  14.6 us (3%)
  matrix products  9.27 us (2%)
    unnamed x3, waiting for transfers between devices  270 us
    all_gather x1, waiting for transfers between devices, project_keys(): lax.all_gather(key_weight, ('dp', 'seq'), axis=0, tiled=True)  31.5 us
    all_to_all x1, waiting for transfers between devices, side_by_side(): lax.all_to_all(both, axis, split_axis=split_dim, concat_axis=concat_dim,...  25.2 us
    ppermute x6, starting transfers between devices, shifted(): return lax.ppermute(shard, axis, pairs)  20.3 us
    reduce_sum x1, other arithmetic, block_targets(): table = jnp.sum(jnp.where(matches, label_prob[..., None], 0.0), axis=2)  13.4 us
    all_to_all x1, starting transfers between devices, move_rows(): lax.all_to_all(row_places, 'seq', split_axis=0, concat_axis=0, tiled=True)  13.2 us
    ppermute x6, waiting for transfers between devices, shifted(): return lax.ppermute(shard, axis, pairs)  10.8 us
  transfers between devices with their start and end apart: 10, of which 8 were waited for; matrix products, arithmetic and copies ran while one was open for 12% of the time, Pallas kernels for 0%

commit v1 on v0

v1 whole, which is shorter than its diff:
```python
import jax
import jax.numpy as jnp
import numpy as np
from jax import lax
from jax.sharding import Mesh
from jax.sharding import PartitionSpec as P

HEAD_DIM = 128
SPAN = 2
SLOTS = 6

negative = -1e30
rope_base = 500000.0

SEQ = ("z", "xh", "xl")
EVERY = ("y", "core") + SEQ


def exchange(pieces, axes):
    return lax.all_to_all(pieces, axes, split_axis=0, concat_axis=0, tiled=True)


def seq_shift(shard, by):
    devices = lax.axis_size(SEQ)
    pairs = [(i, i + by) for i in range(devices) if 0 <= i + by < devices]
    return lax.ppermute(shard, SEQ, pairs)


def core_swap(shard):
    return lax.ppermute(shard, "core", [(0, 1), (1, 0)])


def turn_angles(positions):
    halfway = HEAD_DIM // 2
    frequency = rope_base ** (-2.0 * jnp.arange(halfway, dtype=jnp.float32) / HEAD_DIM)
    angle = positions.astype(jnp.float32)[:, None] * frequency[None, :]
    return jnp.cos(angle)[:, None, :], jnp.sin(angle)[:, None, :]


def rotate(matrix, cosine, sine):
    count = matrix.shape[0]
    halfway = HEAD_DIM // 2
    split = matrix.reshape(count, -1, HEAD_DIM)
    first_half = split[..., :halfway]
    second_half = split[..., halfway:]
    joined = jnp.concatenate(
        [first_half * cosine - second_half * sine, second_half * cosine + first_half * sine],
        axis=-1,
    )
    return joined.reshape(count, -1)


def dialogue_starts(lengths, positions):
    ending = jnp.cumsum(lengths)
    picked = jnp.where(ending[None, :] <= positions[:, None], lengths[None, :], 0)
    return jnp.sum(picked, axis=1)


def block_targets(label_index, label_prob, key_start, width):
    within = label_index - key_start
    columns = jnp.arange(width, dtype=jnp.int32)
    matches = within[..., None] == columns[None, None, None, :]
    table = jnp.sum(jnp.where(matches, label_prob[..., None], 0.0), axis=2)
    return jnp.transpose(table, (1, 0, 2))


def weight_pieces(key_weight):
    rows, columns = key_weight.shape
    lines = lax.axis_size("y")
    got = exchange(jnp.broadcast_to(key_weight, (2 * lines, rows, columns)), ("y", "xl"))
    tiles = got.reshape(lines, 2 * rows, columns)
    half = lines // 2
    mine = lax.dynamic_slice_in_dim(tiles, lax.axis_index("xl") * half, half, 0)
    return jnp.transpose(mine, (1, 0, 2)).reshape(2 * rows, half * columns)


def local(
    hidden, queries, values, row_target, key_weight, dialogue_lengths, teacher_pick, teacher_prob
):
    bf16, f32 = jnp.bfloat16, jnp.float32
    local_rows, width = hidden.shape
    seq_count = lax.axis_size(SEQ)
    seq_index = lax.axis_index(SEQ)
    lines = lax.axis_size("y")
    device_count = seq_count * lines * lax.axis_size("core")
    head_count = queries.shape[1] // HEAD_DIM
    kv_width = values.shape[1]
    kv_count = kv_width // HEAD_DIM
    group_size = head_count // kv_count
    top_count = teacher_pick.shape[1] // head_count
    scaling = HEAD_DIM ** (-0.5)

    destination = row_target // local_rows
    offset_in = row_target - destination * local_rows
    order = jnp.arange(local_rows, dtype=jnp.int32)
    earlier = (destination[None, :] == destination[:, None]) & (order[None, :] < order[:, None])
    rank_in = jnp.sum(earlier.astype(jnp.int32), axis=1)
    tiles = (2 * width + kv_width) // HEAD_DIM
    extra = tiles // 4
    main = tiles - extra
    rows_all = jnp.concatenate([hidden, queries, values], axis=1)
    parcel_row = jnp.arange(seq_count * 8, dtype=jnp.int32)
    block_of, place = parcel_row // 8, parcel_row % 8
    to_block = destination[None, :] == block_of[:, None]
    low = to_block & (place[:, None] == rank_in[None, :]) & (place[:, None] < SLOTS)
    packed = []
    metas = []
    for m in range(3):
        high = to_block & (place[:, None] - SLOTS + 2 * m == rank_in[None, :]) & (place[:, None] >= SLOTS)
        select = jnp.concatenate([low, high], axis=1).astype(bf16)
        left = rows_all[:, : main * HEAD_DIM].reshape(local_rows, main // 3, 3, HEAD_DIM)[:, :, m]
        left = left.reshape(local_rows, main // 3 * HEAD_DIM)
        both = jnp.concatenate([left, rows_all[:, main * HEAD_DIM :]], axis=0)
        packed.append(jnp.dot(select, both, preferred_element_type=f32).astype(bf16))
        shifted = (offset_in - local_rows).astype(f32)
        meta = jnp.sum(jnp.where(low | high, shifted[None, :], 0.0), axis=1) + local_rows
        metas.append(meta)
    body = jnp.stack([p.reshape(-1, main // 3, HEAD_DIM) for p in packed], axis=2).reshape(
        -1, main * HEAD_DIM
    )
    lane = jnp.arange(HEAD_DIM, dtype=jnp.int32)[None, :]
    meta_tile = jnp.where(
        lane == 0, metas[0][:, None], jnp.where(lane == 1, metas[1][:, None], metas[2][:, None])
    ).astype(bf16)
    passed_on = weight_pieces(key_weight)
    payload = jnp.concatenate(
        [
            jnp.concatenate([body, meta_tile], axis=1).reshape(seq_count, 8, -1),
            jnp.broadcast_to(passed_on[None], (seq_count,) + passed_on.shape),
        ],
        axis=2,
    )
    received = exchange(payload, SEQ)

    flat = received.reshape(seq_count * 8, -1)
    meta_got = flat[:, main * HEAD_DIM : main * HEAD_DIM + 3].astype(f32)
    token = jnp.arange(local_rows, dtype=f32)
    is_low = place < SLOTS
    mains, extras = [], 0.0
    for m in range(3):
        hit = meta_got[:, m][None, :] == token[:, None]
        select = jnp.concatenate([hit & is_low[None, :], hit & ~is_low[None, :]], axis=0).astype(bf16)
        part = flat[:, : main * HEAD_DIM].reshape(-1, main // 3, 3, HEAD_DIM)[:, :, m]
        part = part.reshape(seq_count * 8, -1)
        done = jnp.dot(select, part, preferred_element_type=f32)
        mains.append(done[:local_rows].astype(bf16).reshape(local_rows, main // 3, HEAD_DIM))
        extras = extras + done[local_rows:]
    rows_seq = jnp.concatenate(
        [jnp.stack(mains, axis=2).reshape(local_rows, -1), extras.astype(bf16)], axis=1
    )
    hidden_seq = rows_seq[:, :width]
    queries_seq = rows_seq[:, width : 2 * width]
    values_seq = rows_seq[:, 2 * width :]

    half = lines // 2
    weight_got = received[:, :, (main + 1) * HEAD_DIM :].reshape(
        seq_count // 2, 2, 8, half, kv_width
    )
    own_half = jnp.transpose(weight_got, (1, 3, 0, 2, 4)).reshape(lines, local_rows, kv_width)
    other_half = core_swap(own_half)
    core = lax.axis_index("core")
    first = jnp.where(core == 0, own_half, other_half)
    second = jnp.where(core == 0, other_half, own_half)
    weight = jnp.stack([first, second], axis=1).reshape(width, kv_width)

    positions = seq_index * local_rows + jnp.arange(local_rows, dtype=jnp.int32)
    cosine, sine = turn_angles(positions)
    keys_seq = rotate(
        jnp.dot(hidden_seq, weight, preferred_element_type=f32), cosine, sine
    ).astype(bf16)
    starts = dialogue_starts(dialogue_lengths[0], positions)
    reach = (positions - starts + 1)[:, None]
    label_index = (starts[:, None] + teacher_pick % reach).reshape(
        local_rows, head_count, top_count
    )
    label_prob = teacher_prob.reshape(local_rows, head_count, top_count)
    target_mass = jnp.sum(label_prob, axis=2).T.reshape(kv_count, group_size, local_rows)
    entropy = jnp.sum(label_prob * jnp.log(label_prob), axis=(1, 2))
    query_heads = queries_seq.reshape(local_rows, kv_count, group_size, HEAD_DIM)
    blocks = [(keys_seq, values_seq)]
    for distance in range(1, SPAN + 1):
        blocks.append((seq_shift(keys_seq, distance), seq_shift(values_seq, distance)))

    def scores_of(key_block, key_start):
        key_heads = key_block.reshape(local_rows, kv_count, HEAD_DIM)
        score = (
            jnp.einsum("tkgd,wkd->kgtw", query_heads, key_heads, preferred_element_type=f32)
            * scaling
        )
        key_pos = key_start + jnp.arange(local_rows, dtype=jnp.int32)
        allowed = (key_pos[None, :] >= starts[:, None]) & (key_pos[None, :] <= positions[:, None])
        held = jnp.where(allowed[None, None], score, negative)
        table = block_targets(label_index, label_prob, key_start, local_rows)
        return (score, held, table.reshape(kv_count, group_size, local_rows, local_rows))

    tops, totals, pickings = ([], [], [])
    for distance, (key_block, value_block) in enumerate(blocks):
        key_start = (seq_index - distance) * local_rows
        score, held, table = scores_of(key_block, key_start)
        block_top = jnp.max(held, axis=-1)
        tops.append(block_top)
        totals.append(jnp.sum(jnp.exp(held - block_top[..., None]), axis=-1))
        pickings.append(jnp.sum(table * score, axis=-1))
    top_all = jnp.max(jnp.stack(tops), axis=0)
    total_all = jnp.sum(jnp.stack(totals) * jnp.exp(jnp.stack(tops) - top_all[None]), axis=0)
    lse = top_all + jnp.log(total_all)
    picked_all = jnp.sum(jnp.stack(pickings), axis=0)
    token_loss = (
        entropy - jnp.sum(picked_all, axis=(0, 1)) + jnp.sum(target_mass * lse, axis=(0, 1))
    ) / head_count

    output_sum = jnp.zeros((local_rows, kv_count, group_size, HEAD_DIM), f32)
    block_grads = []
    for distance, (key_block, value_block) in enumerate(blocks):
        key_start = (seq_index - distance) * local_rows
        score, held, table = scores_of(key_block, key_start)
        weight_of = jnp.exp(held - lse[..., None])
        value_heads = value_block.reshape(local_rows, kv_count, HEAD_DIM)
        output_sum = output_sum + jnp.einsum(
            "kgtw,wkd->tkgd", weight_of.astype(bf16), value_heads, preferred_element_type=f32
        )
        slope = ((weight_of * target_mass[..., None] - table) / head_count).astype(bf16)
        gradient = (
            jnp.einsum("kgtw,tkgd->wkd", slope, query_heads, preferred_element_type=f32) * scaling
        )
        block_grads.append(gradient.reshape(local_rows, kv_count * HEAD_DIM))
    attn_out = output_sum.astype(bf16).reshape(local_rows, head_count * HEAD_DIM)
    rotated_grad = block_grads[0]
    for distance in range(1, SPAN + 1):
        rotated_grad = rotated_grad + seq_shift(
            block_grads[distance].astype(bf16), -distance
        ).astype(f32)
    key_grad = rotate(rotated_grad, cosine, -sine).astype(bf16)

    inverse_root = (local_rows * device_count) ** (-0.5)
    hidden_tiles = hidden_seq.reshape(local_rows, lines, 2, HEAD_DIM)
    mine = jnp.where(core == 0, hidden_tiles[:, :, 0], hidden_tiles[:, :, 1])
    theirs = jnp.where(core == 0, hidden_tiles[:, :, 1], hidden_tiles[:, :, 0])

    def term(tiles_of):
        return jnp.einsum(
            "td,tc->dc", tiles_of.reshape(local_rows, -1), key_grad, preferred_element_type=f32
        )

    from_other = core_swap(term(theirs).astype(bf16))
    summed = (term(mine) + from_other.astype(f32)).astype(bf16)
    pieces = jnp.transpose(
        summed.reshape(2, half, seq_count // 2, 8, kv_width), (2, 0, 3, 1, 4)
    ).reshape(seq_count, 8, half * kv_width)
    plane = jnp.sum(exchange(pieces, SEQ).astype(f32), axis=0)
    plane = jnp.transpose(plane.reshape(2, 4, half, kv_width), (2, 0, 1, 3))
    side = lax.axis_index("xl")
    empty = jnp.zeros_like(plane)
    last = jnp.stack([jnp.where(side == 0, plane, empty), jnp.where(side == 1, plane, empty)])
    weight_grad = jnp.sum(
        exchange(last.reshape(2 * lines, 4, kv_width), ("y", "xl")), axis=0
    ) * inverse_root
    return (attn_out, token_loss, weight_grad)


def solution(mesh):
    fine = Mesh(np.asarray(mesh.devices).reshape(8, 2, 8, 2, 2), EVERY)
    pack = ("y", "core")
    placed = (
        P(EVERY, None),
        P(EVERY, None),
        P(EVERY, None),
        P(EVERY),
        P(EVERY, None),
        P(pack, None),
        P(EVERY, None),
        P(EVERY, None),
    )
    return jax.shard_map(
        local,
        mesh=fine,
        in_specs=placed,
        out_specs=(P(EVERY, None), P(EVERY), P(EVERY, None)),
        check_vma=False,
    )
```

time: 469 us -> 237 us (0.51)
  the two profiles are of different devices: /device:TPU:24 before, /device:TPU:64 now
where the time goes in v1:
time: 237 us; the launch traced here: 235 us
  waiting for transfers between devices  77.7 us (33%)
  starting transfers between devices  61.2 us (26%)
  local copies, waits for them, and re-layouts  56.1 us (24%)
  other arithmetic  30 us (13%)
  matrix products  9 us (4%)
    all_to_all x4, waiting for transfers between devices, exchange(): return lax.all_to_all(pieces, axes, split_axis=0, concat_axis=0, tiled=True)  45 us
    all_to_all x4, starting transfers between devices, exchange(): return lax.all_to_all(pieces, axes, split_axis=0, concat_axis=0, tiled=True)  35.3 us
    ppermute x6, waiting for transfers between devices, seq_shift(): return lax.ppermute(shard, SEQ, pairs)  30.1 us
    ppermute x6, starting transfers between devices, seq_shift(): return lax.ppermute(shard, SEQ, pairs)  22 us
    reduce_sum x1, other arithmetic, block_targets(): table = jnp.sum(jnp.where(matches, label_prob[..., None], 0.0), axis=2)  13.5 us
    unnamed x42, local copies, waits for them, and re-layouts  9.79 us
    transpose x3, local copies, waits for them, and re-layouts, block_targets(): return jnp.transpose(table, (1, 0, 2))  7.75 us
  transfers between devices with their start and end apart: 12, of which 8 were waited for; matrix products, arithmetic and copies ran while one was open for 24% of the time, Pallas kernels for 0%

profile of v1, /device:TPU:64, one launch (start us, length us, event | category | flops | bytes accessed | tf_op | source)
XLA Modules:
  0.0 235.5 jit_solution(9991695592934560183)
XLA Ops:
  0.6 1.3 broadcast_in_dim.257
  2.0 8.1 %all-to-all-start = ((bf16[16,4,512]{2,1,0:T(4,128)(2,1)}), bf16[16,4,512]{2,1,0:T(4,128)(2,1)S(1)}, u32[]{:S(2)}, u32[]{:S(2)}) async-start(bf16[16,4,512]{2,1,0:T(4,128)(2,1)} %broadcast_in_dim.257), calls=%async_computation | async-start | bytes 131072 | tf_op jit(solution)/shard_map/all_to_all | solution.py:20
  11.0 1.3 copy.127
  12.4 1.3 copy.126
  16.9 1.4 pad_maximum_fusion.2
  18.3 4.3 %copy.133 = bf16[256,9,3,128]{3,2,1,0:T(4,128)(2,1)S(1)} copy(bf16[256,9,3,128]{0,3,1,2:T(8,128)(2,1)} %pad_maximum_fusion.2) | data formatting | bytes 3538944 | tf_op jit(solution)/shard_map/stack | solution.py:118
  22.7 2.7 %concatenate.60 = bf16[32,8,3456]{2,1,0:T(8,128)(2,1)} reshape(bf16[256,9,3,128]{3,2,1,0:T(4,128)(2,1)S(1)} %copy.133) | data formatting | bytes 3538944 | tf_op jit(solution)/shard_map/concatenate | solution.py:128
  26.5 3.3 %pad_maximum_fusion = bf16[32,8,5632]{2,1,0:T(8,128)(2,1)} fusion(bf16[32,8,2048]{2,1,0:T(8,128)(2,1)S(1)} %broadcast_in_dim.259, bf16[32,8,128]{2,1,0:T(8,128)(2,1)S(1)} %select_convert_fusion, bf16[32,8,3456]{2,1,0:T(8,128)(2,1)} %concatenate.60), kind=kLoop, calls=%fused_computation.6 | loop fusion | flops 8650752 | bytes 5767168 | tf_op jit(solution)/shard_map/concatenate | solution.py:126
  29.8 12.9 %all-to-all-start.1 = ((bf16[32,8,5632]{2,1,0:T(8,128)(2,1)}), bf16[32,8,5632]{2,1,0:T(8,128)(2,1)S(1)}, u32[]{:S(2)}, u32[]{:S(2)}) async-start(bf16[32,8,5632]{2,1,0:T(8,128)(2,1)} %pad_maximum_fusion), calls=%async_computation.1 | async-start | bytes 5767168 | tf_op jit(solution)/shard_map/all_to_all | solution.py:20
  44.0 1.4 copy.159
  45.3 1.4 copy.163
  46.7 1.4 copy.165
  48.2 1.4 copy.161
  49.6 13.5 %select_reduce_fusion.1 = (f32[128,16,128]{2,1,0:T(8,128)}, f32[128,16,128]{2,1,0:T(8,128)}, f32[128,16,128]{2,1,0:T(8,128)}) fusion(s32[128,16,8]{2,1,0:T(8,128)} %copy.163, f32[128,16,8]{2,1,0:T(8,128)} %copy.161, s32[128,16,8]{2,1,0:T(8,128)} %copy.165, s32[128,16,8]{2,1,0:T(8,128)} %copy.159), kind=kLoop, calls=%fused_computation.2 | loop fusion | flops 18087936 | bytes 3407872 | tf_op jit(solution)/shard_map/reduce_sum | solution.py:63
  63.0 2.6 %copy.162 = f32[16,128,128]{1,2,0:T(8,128)} copy(f32[16,128,128]{2,0,1:T(8,128)} %bitcast.208) | data formatting | bytes 2097152 | tf_op jit(solution)/shard_map/transpose | solution.py:64
  65.6 2.6 %copy.164 = f32[16,128,128]{1,2,0:T(8,128)} copy(f32[16,128,128]{2,0,1:T(8,128)} %bitcast.207) | data formatting | bytes 2097152 | tf_op jit(solution)/shard_map/transpose | solution.py:64
  68.2 2.6 %copy.166 = f32[16,128,128]{1,2,0:T(8,128)} copy(f32[16,128,128]{2,0,1:T(8,128)} %bitcast.206) | data formatting | bytes 2097152 | tf_op jit(solution)/shard_map/transpose | solution.py:64
  71.8 36.8 %all-to-all-done.1 = bf16[32,8,5632]{2,1,0:T(8,128)(2,1)S(1)} async-done(((bf16[32,8,5632]{2,1,0:T(8,128)(2,1)}), bf16[32,8,5632]{2,1,0:T(8,128)(2,1)S(1)}, u32[]{:S(2)}, u32[]{:S(2)}) %all-to-all-start.1) | async-done | bytes 2883616 | tf_op jit(solution)/shard_map/all_to_all | solution.py:20
  108.6 1.3 slice.134
  110.1 3.9 %copy.203 = bf16[256,3456]{0,1:T(8,128)(2,1)} copy(bf16[256,3456]{1,0:T(8,128)(2,1)} %slice.134) | data formatting | bytes 3538944
  113.9 1.5 fusion.106
  119.1 1.1 slice.148
  120.2 1.9 reshape.613
  122.3 1.9 collective-permute-start
  124.7 1.2 copy.139
  127.2 1.4 select_bitcast_fusion.1
  128.8 1.5 copy.143
  130.3 4.0 %copy.144 = bf16[512,2048]{1,0:T(8,128)(2,1)} copy(bf16[512,2048]{0,1:T(8,128)(2,1)} %bitcast.202) | data formatting | bytes 4194304 | tf_op jit(solution)/shard_map/dot_general | solution.py:169
  134.3 2.3 fusion.23
  136.7 3.5 %collective-permute-start.1 = (bf16[128,512]{0,1:T(8,128)(2,1)S(1)}, bf16[128,512]{0,1:T(8,128)(2,1)S(1)}, u32[]{:S(2)}, u32[]{:S(2)}) collective-permute-start(bf16[128,512]{0,1:T(8,128)(2,1)S(1)} %bitcast.257), channel_id=1, source_target_pairs={{0,1},{1,2},{2,3},{3,4},{4,5},{5,6},{6,7},{7,8},{8,9},{9,10},{10,1... | collective-permute-start | bytes 393224 | tf_op jit(solution)/shard_map/ppermute | solution.py:26
  140.2 4.8 %collective-permute-start.2 = (bf16[128,512]{0,1:T(8,128)(2,1)S(1)}, bf16[128,512]{0,1:T(8,128)(2,1)S(1)}, u32[]{:S(2)}, u32[]{:S(2)}) collective-permute-start(bf16[128,512]{0,1:T(8,128)(2,1)S(1)} %bitcast.258), channel_id=1, source_target_pairs={{0,2},{1,3},{2,4},{3,5},{4,6},{5,7},{6,8},{7,9},{8,10},{9,11},{10,... | collective-permute-start | bytes 393224 | tf_op jit(solution)/shard_map/ppermute | solution.py:26
  147.1 3.0 %collective-permute-done.2 = bf16[128,512]{0,1:T(8,128)(2,1)S(1)} collective-permute-done((bf16[128,512]{0,1:T(8,128)(2,1)S(1)}, bf16[128,512]{0,1:T(8,128)(2,1)S(1)}, u32[]{:S(2)}, u32[]{:S(2)}) %collective-permute-start.2) | collective-permute-done | bytes 131104 | tf_op jit(solution)/shard_map/ppermute | solution.py:26
  153.3 3.7 %collective-permute-start.5 = (bf16[128,512]{0,1:T(8,128)(2,1)S(1)}, bf16[128,512]{0,1:T(8,128)(2,1)S(1)}, u32[]{:S(2)}, u32[]{:S(2)}) collective-permute-start(bf16[128,512]{0,1:T(8,128)(2,1)S(1)} %bitcast.255), channel_id=1, source_target_pairs={{1,0},{2,1},{3,2},{4,3},{5,4},{6,5},{7,6},{8,7},{9,8},{10,9},{11,1... | collective-permute-start | bytes 393224 | tf_op jit(solution)/shard_map/ppermute | solution.py:26
  157.0 2.1 collective-permute-start.6
  160.3 5.1 %collective-permute-done.6 = bf16[128,512]{0,1:T(8,128)(2,1)S(1)} collective-permute-done((bf16[128,512]{0,1:T(8,128)(2,1)S(1)}, bf16[128,512]{0,1:T(8,128)(2,1)S(1)}, u32[]{:S(2)}, u32[]{:S(2)}) %collective-permute-start.6) | collective-permute-done | bytes 131104 | tf_op jit(solution)/shard_map/ppermute | solution.py:26
  166.0 1.9 collective-permute-start.7
  168.0 2.6 %collective-permute-done.7 = bf16[1024,512]{1,0:T(8,128)(2,1)S(1)} collective-permute-done((bf16[1024,512]{1,0:T(8,128)(2,1)S(1)}, bf16[1024,512]{1,0:T(8,128)(2,1)S(1)}, u32[]{:S(2)}, u32[]{:S(2)}) %collective-permute-start.7) | collective-permute-done | bytes 1048608 | tf_op jit(solution)/shard_map/ppermute | solution.py:30
  171.9 1.6 reshape.629
  173.5 7.6 %all-to-all-start.2 = ((bf16[32,8,2048]{2,1,0:T(8,128)(2,1)}), bf16[32,8,2048]{2,1,0:T(8,128)(2,1)}, u32[]{:S(2)}, u32[]{:S(2)}) async-start(bf16[32,8,2048]{2,1,0:T(8,128)(2,1)} %reshape.629), calls=%async_computation.2 | async-start | bytes 2097152 | tf_op jit(solution)/shard_map/all_to_all | solution.py:20
  181.7 3.4 %collective-permute-start.3 = (bf16[128,512]{1,0:T(8,128)(2,1)}, bf16[128,512]{1,0:T(8,128)(2,1)}, u32[]{:S(2)}, u32[]{:S(2)}) collective-permute-start(bf16[128,512]{1,0:T(8,128)(2,1)} %slice.143), channel_id=1, source_target_pairs={{0,1},{1,2},{2,3},{3,4},{4,5},{5,6},{6,7},{7,8},{8,9},{9,10},{10,1... | collective-permute-start | bytes 393224 | tf_op jit(solution)/shard_map/ppermute | solution.py:26
  185.1 4.6 %collective-permute-start.4 = (bf16[128,512]{1,0:T(8,128)(2,1)}, bf16[128,512]{1,0:T(8,128)(2,1)}, u32[]{:S(2)}, u32[]{:S(2)}) collective-permute-start(bf16[128,512]{1,0:T(8,128)(2,1)} %slice.143), channel_id=1, source_target_pairs={{0,2},{1,3},{2,4},{3,5},{4,6},{5,7},{6,8},{7,9},{8,10},{9,11},{10,... | collective-permute-start | bytes 393224 | tf_op jit(solution)/shard_map/ppermute | solution.py:26
  190.6 1.0 copy.193
  191.7 20.1 %collective-permute-done.3 = bf16[128,512]{1,0:T(8,128)(2,1)} collective-permute-done((bf16[128,512]{1,0:T(8,128)(2,1)}, bf16[128,512]{1,0:T(8,128)(2,1)}, u32[]{:S(2)}, u32[]{:S(2)}) %collective-permute-start.3) | collective-permute-done | bytes 131104 | tf_op jit(solution)/shard_map/ppermute | solution.py:26
  211.8 1.0 copy.200
  212.8 1.7 copy.201
  216.1 1.4 convert_reduce_fusion
  218.4 6.7 %all-to-all-start.3 = ((f32[16,4,512]{2,1,0:T(4,128)}), f32[16,4,512]{2,1,0:T(4,128)S(1)}, u32[]{:S(2)}, u32[]{:S(2)}) async-start(f32[16,4,512]{2,1,0:T(4,128)} %bitcast.93), calls=%async_computation.3 | async-start | bytes 262144 | tf_op jit(solution)/shard_map/all_to_all | solution.py:20
  226.7 8.2 %all-to-all-done.3 = f32[16,4,512]{2,1,0:T(4,128)S(1)} async-done(((f32[16,4,512]{2,1,0:T(4,128)}), f32[16,4,512]{2,1,0:T(4,128)S(1)}, u32[]{:S(2)}, u32[]{:S(2)}) %all-to-all-start.3) | async-done | bytes 131104 | tf_op jit(solution)/shard_map/all_to_all | solution.py:20
  (142 shorter events, 27.7 us)
Async XLA Ops:
  2.0 24.4 %all-to-all-start = ((bf16[16,4,512]{2,1,0:T(4,128)(2,1)}), bf16[16,4,512]{2,1,0:T(4,128)(2,1)S(1)}, u32[]{:S(2)}, u32[]{:S(2)}) async-start(bf16[16,4,512]{2,1,0:T(4,128)(2,1)} %broadcast_in_dim.257), calls=%async_computation | async-start | bytes 131072 | tf_op jit(solution)/shard_map/all_to_all | solution.py:20
  13.7 0.9 copy-start.13
  29.8 12.9 %copy-start.16 = (s32[1,64]{1,0:T(1,128)S(1)}, s32[1,64]{1,0:T(1,128)}, u32[]{:S(2)}) copy-start(s32[1,64]{1,0:T(1,128)} %param.13) | copy-start | bytes 772
  29.8 13.2 %copy-start.14 = (s32[128,128]{1,0:T(8,128)S(1)}, s32[128,128]{1,0:T(8,128)}, u32[]{:S(2)}) copy-start(s32[128,128]{1,0:T(8,128)} %param.14) | copy-start | bytes 196612
  29.8 78.8 %all-to-all-start.1 = ((bf16[32,8,5632]{2,1,0:T(8,128)(2,1)}), bf16[32,8,5632]{2,1,0:T(8,128)(2,1)S(1)}, u32[]{:S(2)}, u32[]{:S(2)}) async-start(bf16[32,8,5632]{2,1,0:T(8,128)(2,1)} %pad_maximum_fusion), calls=%async_computation.1 | async-start | bytes 5767168 | tf_op jit(solution)/shard_map/all_to_all | solution.py:20
  43.3 4.9 %copy-start.10 = (f32[128,128]{1,0:T(8,128)S(1)}, f32[128,128]{1,0:T(8,128)}, u32[]{:S(2)}) copy-start(f32[128,128]{1,0:T(8,128)} %param.15) | copy-start | bytes 196612
  120.2 4.0 %copy-start.5 = (bf16[128,1152]{1,0:T(8,128)(2,1)S(1)}, bf16[128,1152]{1,0:T(8,128)(2,1)}, u32[]{:S(2)}) copy-start(bf16[128,1152]{1,0:T(8,128)(2,1)} %slice.179) | copy-start | bytes 884740
  122.1 2.4 %copy-start.6 = (bf16[128,1152]{1,0:T(8,128)(2,1)S(1)}, bf16[128,1152]{1,0:T(8,128)(2,1)}, u32[]{:S(2)}) copy-start(bf16[128,1152]{1,0:T(8,128)(2,1)} %slice.178) | copy-start | bytes 884740
  122.3 4.9 %collective-permute-start = (bf16[8,128,512]{2,1,0:T(8,128)(2,1)S(1)}, bf16[8,128,512]{2,1,0:T(8,128)(2,1)}, u32[]{:S(2)}, u32[]{:S(2)}) collective-permute-start(bf16[8,128,512]{2,1,0:T(8,128)(2,1)S(1)} %bitcast.204), channel_id=1, source_target_pairs={{0,32},{32,0},{1,33},{33,1},{2,34},{34,2},{3,35},{35,3},{4,36},{36... | collective-permute-start | bytes 3145736 | tf_op jit(solution)/shard_map/ppermute | solution.py:30
  134.3 2.3 copy-start.12
  136.6 8.8 %copy-start.4 = (f32[16,128,128]{1,2,0:T(8,128)S(1)}, f32[16,128,128]{1,2,0:T(8,128)}, u32[]{:S(2)}) copy-start(f32[16,128,128]{1,2,0:T(8,128)} %copy.162) | copy-start | bytes 3145732
  136.7 10.0 %collective-permute-start.1 = (bf16[128,512]{0,1:T(8,128)(2,1)S(1)}, bf16[128,512]{0,1:T(8,128)(2,1)S(1)}, u32[]{:S(2)}, u32[]{:S(2)}) collective-permute-start(bf16[128,512]{0,1:T(8,128)(2,1)S(1)} %bitcast.257), channel_id=1, source_target_pairs={{0,1},{1,2},{2,3},{3,4},{4,5},{5,6},{6,7},{7,8},{8,9},{9,10},{10,1... | collective-permute-start | bytes 393224 | tf_op jit(solution)/shard_map/ppermute | solution.py:26
  140.2 9.9 %collective-permute-start.2 = (bf16[128,512]{0,1:T(8,128)(2,1)S(1)}, bf16[128,512]{0,1:T(8,128)(2,1)S(1)}, u32[]{:S(2)}, u32[]{:S(2)}) collective-permute-start(bf16[128,512]{0,1:T(8,128)(2,1)S(1)} %bitcast.258), channel_id=1, source_target_pairs={{0,2},{1,3},{2,4},{3,5},{4,6},{5,7},{6,8},{7,9},{8,10},{9,11},{10,... | collective-permute-start | bytes 393224 | tf_op jit(solution)/shard_map/ppermute | solution.py:26
  145.4 13.6 %copy-start = (f32[4,4,128,128]{2,3,1,0:T(8,128)}, f32[4,4,128,128]{2,3,1,0:T(8,128)S(1)}, u32[]{:S(2)}) copy-start(f32[4,4,128,128]{2,3,1,0:T(8,128)S(1)} %get-tuple-element.82) | copy-start | bytes 3145732
  145.7 4.8 %copy-start.2 = (f32[16,128,128]{1,2,0:T(8,128)S(1)}, f32[16,128,128]{1,2,0:T(8,128)}, u32[]{:S(2)}) copy-start(f32[16,128,128]{1,2,0:T(8,128)} %copy.164) | copy-start | bytes 3145732
  150.1 1.2 copy-start.3
  153.3 7.1 %collective-permute-start.5 = (bf16[128,512]{0,1:T(8,128)(2,1)S(1)}, bf16[128,512]{0,1:T(8,128)(2,1)S(1)}, u32[]{:S(2)}, u32[]{:S(2)}) collective-permute-start(bf16[128,512]{0,1:T(8,128)(2,1)S(1)} %bitcast.255), channel_id=1, source_target_pairs={{1,0},{2,1},{3,2},{4,3},{5,4},{6,5},{7,6},{8,7},{9,8},{10,9},{11,1... | collective-permute-start | bytes 393224 | tf_op jit(solution)/shard_map/ppermute | solution.py:26
  157.0 8.6 %copy-start.11 = (f32[128,64]{0,1:T(8,128)S(1)}, f32[128,64]{0,1:T(8,128)}, u32[]{:S(2)}) copy-start(f32[128,64]{0,1:T(8,128)} %get-tuple-element.61) | copy-start | bytes 98308
  157.0 8.6 %copy-start.8 = (bf16[128,8,1,128]{0,3,1,2:T(8,128)(2,1)S(1)}, bf16[128,8,1,128]{0,3,1,2:T(8,128)(2,1)}, u32[]{:S(2)}) copy-start(bf16[128,8,1,128]{0,3,1,2:T(8,128)(2,1)} %get-tuple-element.41) | copy-start | bytes 786436
  157.0 8.5 %collective-permute-start.6 = (bf16[128,512]{0,1:T(8,128)(2,1)S(1)}, bf16[128,512]{0,1:T(8,128)(2,1)S(1)}, u32[]{:S(2)}, u32[]{:S(2)}) collective-permute-start(bf16[128,512]{0,1:T(8,128)(2,1)S(1)} %bitcast.254), channel_id=1, source_target_pairs={{2,0},{3,1},{4,2},{5,3},{6,4},{7,5},{8,6},{9,7},{10,8},{11,9},{12,... | collective-permute-start | bytes 393224 | tf_op jit(solution)/shard_map/ppermute | solution.py:26
  159.5 11.1 %copy-start.7 = (bf16[128,8,1,128]{0,3,1,2:T(8,128)(2,1)S(1)}, bf16[128,8,1,128]{0,3,1,2:T(8,128)(2,1)}, u32[]{:S(2)}) copy-start(bf16[128,8,1,128]{0,3,1,2:T(8,128)(2,1)} %get-tuple-element.42) | copy-start | bytes 786436
  166.0 4.6 %collective-permute-start.7 = (bf16[1024,512]{1,0:T(8,128)(2,1)S(1)}, bf16[1024,512]{1,0:T(8,128)(2,1)S(1)}, u32[]{:S(2)}, u32[]{:S(2)}) collective-permute-start(bf16[1024,512]{1,0:T(8,128)(2,1)S(1)} %convolution_convert_fusion.3), channel_id=1, source_target_pairs={{0,32},{32,0},{1,33},{33,1},{2,34},{34,2},{3,35},{35,3},{4,36},{36... | collective-permute-start | bytes 3145736 | tf_op jit(solution)/shard_map/ppermute | solution.py:30
  173.5 41.0 %copy-start.15 = (f32[4,4,128]{2,1,0:T(4,128)S(1)}, f32[4,4,128]{2,1,0:T(4,128)}, u32[]{:S(2)}) copy-start(f32[4,4,128]{2,1,0:T(4,128)} %get-tuple-element.22) | copy-start | bytes 24580
  173.5 41.1 %copy-start.1 = (f32[4,4,128,128]{2,3,1,0:T(8,128)S(1)}, f32[4,4,128,128]{2,3,1,0:T(8,128)}, u32[]{:S(2)}) copy-start(f32[4,4,128,128]{2,3,1,0:T(8,128)} %copy-done) | copy-start | bytes 3145732
  173.5 42.7 %all-to-all-start.2 = ((bf16[32,8,2048]{2,1,0:T(8,128)(2,1)}), bf16[32,8,2048]{2,1,0:T(8,128)(2,1)}, u32[]{:S(2)}, u32[]{:S(2)}) async-start(bf16[32,8,2048]{2,1,0:T(8,128)(2,1)} %reshape.629), calls=%async_computation.2 | async-start | bytes 2097152 | tf_op jit(solution)/shard_map/all_to_all | solution.py:20
  181.7 30.1 %collective-permute-start.3 = (bf16[128,512]{1,0:T(8,128)(2,1)}, bf16[128,512]{1,0:T(8,128)(2,1)}, u32[]{:S(2)}, u32[]{:S(2)}) collective-permute-start(bf16[128,512]{1,0:T(8,128)(2,1)} %slice.143), channel_id=1, source_target_pairs={{0,1},{1,2},{2,3},{3,4},{4,5},{5,6},{6,7},{7,8},{8,9},{9,10},{10,1... | collective-permute-start | bytes 393224 | tf_op jit(solution)/shard_map/ppermute | solution.py:26
  185.1 27.8 %collective-permute-start.4 = (bf16[128,512]{1,0:T(8,128)(2,1)}, bf16[128,512]{1,0:T(8,128)(2,1)}, u32[]{:S(2)}, u32[]{:S(2)}) collective-permute-start(bf16[128,512]{1,0:T(8,128)(2,1)} %slice.143), channel_id=1, source_target_pairs={{0,2},{1,3},{2,4},{3,5},{4,6},{5,7},{6,8},{7,9},{8,10},{9,11},{10,... | collective-permute-start | bytes 393224 | tf_op jit(solution)/shard_map/ppermute | solution.py:26
  214.9 0.9 copy-start.9
  218.4 16.5 %all-to-all-start.3 = ((f32[16,4,512]{2,1,0:T(4,128)}), f32[16,4,512]{2,1,0:T(4,128)S(1)}, u32[]{:S(2)}, u32[]{:S(2)}) async-start(f32[16,4,512]{2,1,0:T(4,128)} %bitcast.93), calls=%async_computation.3 | async-start | bytes 262144 | tf_op jit(solution)/shard_map/all_to_all | solution.py:20
